TPU v7x, 256 devices: a whole 4x4x8 slice. The times are simulated.
256 devices in a mesh: scene: 8 (over x, core), region: 32 (over z, y).
Axes of the slice: x: 4, y: 4, z: 8, core: 2. Of those that a mesh axis runs over, the one named last changes fastest.
Arguments:
- tiles: bfloat16 [8, 64, 32, 32, 256], P('scene', 'region'), may hold values from -6 to 6
- cotangent: bfloat16 [8, 64, 16, 16, 256], P('scene', 'region'), may hold values from -6 to 6
- positions: int32 [8, 64], P('scene', 'region'), may hold values from 0 to 63, each once within a row
- clear: int32 [8, 64], P('scene', 'region'), may hold values 0 or 1
- w_first: bfloat16 [2304, 256], P('scene'), may hold values from -0.125 to 0.125
- w_second: bfloat16 [2304, 256], P('scene'), may hold values from -0.125 to 0.125
Outputs:
- features: bfloat16 [8, 64, 16, 16, 256], P('scene', 'region')
- grad_first: float32 [2304, 256], P('region', 'scene')
- grad_second: float32 [2304, 256], P('region', 'scene')
Inputs may be any that keep to these rules, and one draw needn't show every extreme that they name: Each scene's row is a permutation of the grid positions 0 to 63.
All inputs are finite; a program needn't handle non-finite values. No bound on the sum of `clear` on one device may be relied on, other than what follows from the above.
Results may differ from a plain program's by a relative error of at most 0.005.
Values may be sent and summed in bfloat16 or wider, within the bound.
A program may use at most 128 MiB of HBM per device.

v0:
```python
import math
import jax
import jax.numpy as jnp
from jax import lax
from jax.sharding import PartitionSpec as P

GW = 4


def silu_slope(pre_act):
    sigmoid_v = jax.nn.sigmoid(pre_act)
    return sigmoid_v * (1.0 + pre_act * (1.0 - sigmoid_v))


def tap_patches(padded, out_side, stride):
    windows = []
    for tap_row in range(3):
        for tap_col in range(3):
            windows.append(
                padded[
                    :,
                    tap_row : tap_row + stride * out_side : stride,
                    tap_col : tap_col + stride * out_side : stride,
                    :,
                ]
            )
    stacked = jnp.concatenate(windows, axis=-1)
    return stacked.reshape(-1, stacked.shape[-1])


def shift_down(values, axis_num):
    widths = [(0, 0)] * values.ndim
    widths[axis_num] = (1, 0)
    padded = jnp.pad(values, widths)
    return lax.slice_in_dim(padded, 0, values.shape[axis_num], 1, axis_num)


def local(tiles, cotangent, positions, clear, w_first, w_second):
    tiles_here = tiles[0]
    slot_count = tiles_here.shape[0]
    tile_side = tiles_here.shape[1]
    tile_half = tile_side // 2
    channels = tiles_here.shape[3]
    local_pos = positions[0]
    every_pos = lax.all_gather(positions, "region", axis=1, tiled=True)[0]
    tile_count = every_pos.shape[0]
    grid_rows = tile_count // GW
    slot_ids = jnp.arange(tile_count, dtype=jnp.int32)
    onehot = (every_pos[:, None] == slot_ids[None, :]).astype(jnp.int32)
    slot_of = jnp.sum(onehot * slot_ids[:, None], axis=0)
    row_here = local_pos // GW
    col_here = local_pos % GW

    def fetch(all_rims, down, sideways, which):
        new_row = row_here + down
        new_col = col_here + sideways
        inside = (new_row >= 0) & (new_row < grid_rows) & (new_col >= 0) & (new_col < GW)
        position = jnp.clip(new_row, 0, grid_rows - 1) * GW + jnp.clip(new_col, 0, GW - 1)
        picked = jnp.take(all_rims, jnp.take(slot_of, position), axis=0)[:, which]
        return picked * inside.astype(picked.dtype)[:, None, None]

    edge_rims = jnp.stack(
        [
            tiles_here[:, 0],
            tiles_here[:, tile_side - 1],
            tiles_here[:, :, 0],
            tiles_here[:, :, tile_side - 1],
        ],
        axis=1,
    )
    all_edges = lax.all_gather(edge_rims, "region", axis=0, tiled=True)
    above_row = fetch(all_edges, -1, 0, 1)
    below_row = fetch(all_edges, 1, 0, 0)
    left_col = fetch(all_edges, 0, -1, 3)
    right_col = fetch(all_edges, 0, 1, 2)
    corner_ul = fetch(all_edges, -1, -1, 1)[:, tile_side - 1]
    corner_ur = fetch(all_edges, -1, 1, 1)[:, 0]
    corner_dl = fetch(all_edges, 1, -1, 0)[:, tile_side - 1]
    corner_dr = fetch(all_edges, 1, 1, 0)[:, 0]
    upper = jnp.concatenate([corner_ul[:, None], above_row, corner_ur[:, None]], axis=1)
    lower = jnp.concatenate([corner_dl[:, None], below_row, corner_dr[:, None]], axis=1)
    middle = jnp.concatenate([left_col[:, :, None], tiles_here, right_col[:, :, None]], axis=2)
    input_pad = jnp.concatenate([upper[:, None], middle, lower[:, None]], axis=1)
    patches_first = tap_patches(input_pad, tile_side, 1)
    pre_flat = jnp.dot(
        patches_first,
        lax.all_gather(w_first, "scene", axis=0, tiled=True),
        preferred_element_type=jnp.float32,
    )
    second_full = lax.all_gather(w_second, "scene", axis=0, tiled=True)
    pre_act = pre_flat.reshape(slot_count, tile_side, tile_side, channels)
    hidden = jax.nn.silu(pre_act).astype(jnp.bfloat16)
    hidden_rims = jnp.stack([hidden[:, tile_side - 1], hidden[:, :, tile_side - 1]], axis=1)
    all_hidden = lax.all_gather(hidden_rims, "region", axis=0, tiled=True)
    hidden_above = fetch(all_hidden, -1, 0, 0)
    hidden_left = fetch(all_hidden, 0, -1, 1)
    hidden_corner = fetch(all_hidden, -1, -1, 0)[:, tile_side - 1]
    hidden_top = jnp.concatenate([hidden_corner[:, None], hidden_above], axis=1)
    hidden_body = jnp.concatenate([hidden_left[:, :, None], hidden], axis=2)
    hidden_pad = jnp.concatenate([hidden_top[:, None], hidden_body], axis=1)
    patches_second = tap_patches(hidden_pad, tile_half, 2)
    out_flat = jnp.dot(patches_second, second_full, preferred_element_type=jnp.float32)
    features = out_flat.astype(jnp.bfloat16).reshape(1, slot_count, tile_half, tile_half, channels)
    masked = cotangent[0] * clear[0].astype(jnp.bfloat16)[:, None, None, None]
    masked_flat = masked.reshape(-1, channels)
    grad_second = lax.dot_general(
        patches_second, masked_flat, (((0,), (0,)), ((), ())), preferred_element_type=jnp.float32
    )
    grad_rims = jnp.stack([masked[:, 0], masked[:, :, 0]], axis=1)
    all_grads = lax.all_gather(grad_rims, "region", axis=0, tiled=True)
    grad_below = fetch(all_grads, 1, 0, 0)
    grad_right = fetch(all_grads, 0, 1, 1)
    grad_corner = fetch(all_grads, 1, 1, 0)[:, 0]
    grad_body = jnp.concatenate([masked, grad_right[:, :, None]], axis=2)
    grad_bottom = jnp.concatenate([grad_below, grad_corner[:, None]], axis=1)
    grad_pad = jnp.concatenate([grad_body, grad_bottom[:, None]], axis=1)
    extended = tile_half + 1
    spread = lax.dot_general(
        grad_pad.reshape(-1, channels),
        second_full,
        (((1,), (1,)), ((), ())),
        preferred_element_type=jnp.float32,
    )
    spread = spread.reshape(slot_count, extended, extended, 3, 3, channels)
    row_even = spread[:, :, :, 0] + shift_down(spread[:, :, :, 2], 1)
    row_odd = spread[:, :, :, 1]
    by_rows = jnp.stack([row_even, row_odd], axis=2).reshape(
        slot_count, 2 * extended, extended, 3, channels
    )
    col_even = by_rows[:, :, :, 0] + shift_down(by_rows[:, :, :, 2], 2)
    col_odd = by_rows[:, :, :, 1]
    dense = jnp.stack([col_even, col_odd], axis=3).reshape(
        slot_count, 2 * extended, 2 * extended, channels
    )
    dhidden = dense[:, 1 : tile_side + 1, 1 : tile_side + 1]
    dpre = (dhidden * silu_slope(pre_act)).astype(jnp.bfloat16)
    grad_first = lax.dot_general(
        patches_first,
        dpre.reshape(-1, channels),
        (((0,), (0,)), ((), ())),
        preferred_element_type=jnp.float32,
    )
    row_block = grad_first.shape[0] // lax.axis_size("region")
    full_first, full_second = lax.psum((grad_first, grad_second), "region")
    sum_sq = jnp.sum(full_first * full_first) + jnp.sum(full_second * full_second)
    row_start = lax.axis_index("region") * row_block
    share_first = lax.dynamic_slice_in_dim(full_first, row_start, row_block, 0)
    share_second = lax.dynamic_slice_in_dim(full_second, row_start, row_block, 0)
    factor = 3.0 * channels * math.sqrt(2.0) / (jnp.sqrt(sum_sq) + 0.01) / lax.axis_size("scene")
    out_first, out_second = (
        lax.psum_scatter(factor * share_first, "scene", scatter_dimension=1, tiled=True),
        lax.psum_scatter(factor * share_second, "scene", scatter_dimension=1, tiled=True),
    )
    return (features, out_first, out_second)


def solution(mesh):
    in_specs = (
        P("scene", "region", None, None, None),
        P("scene", "region", None, None, None),
        P("scene", "region"),
        P("scene", "region"),
        P("scene", None),
        P("scene", None),
    )
    out_specs = (P("scene", "region", None, None, None), P("region", "scene"), P("region", "scene"))
    return jax.shard_map(local, mesh=mesh, in_specs=in_specs, out_specs=out_specs, check_vma=False)
```

profile of v0, /device:TPU:8, one launch (start us, length us, event | category | flops | bytes accessed | tf_op | source)
XLA Modules:
  0.0 681.8 jit_solution(13259119407148330793)
XLA Ops:
  17.6 22.6 %all-reduce.2 = s32[64]{0:T(128)S(1)} all-reduce(s32[64]{0:T(128)S(1)} %bitcast_dynamic-update-slice_fusion), channel_id=1, replica_groups=mesh['scene'=8,'region'=32] {'region'}, use_global_device_ids=true, to_apply=%add.2 | all-reduce | flops 64 | bytes 512
  50.9 37.8 %all-gather.14.cloned.1.call-done = bf16[64,2,16,256]{3,2,1,0:T(8,128)(2,1)} async-done(((bf16[2,2,16,256]{3,2,1,0:T(8,128)(2,1)}), bf16[64,2,16,256]{3,2,1,0:T(8,128)(2,1)}) %all-gather.14.cloned.1.call-update) | async-done | bytes 1048592 | tf_op jit(solution)/shard_map/all_gather | solution.py:110
  94.4 76.7 %all-gather.6.cloned.1.call-done = bf16[64,4,32,256]{3,2,1,0:T(8,128)(2,1)} async-done(((bf16[2,4,32,256]{3,2,1,0:T(8,128)(2,1)}), bf16[64,4,32,256]{3,2,1,0:T(8,128)(2,1)}) %all-gather.6.cloned.1.call-update) | async-done | bytes 4194320 | tf_op jit(solution)/shard_map/all_gather | solution.py:71
  174.6 23.1 %all-gather.12.cloned.1.call-done = bf16[2304,256]{1,0:T(8,128)(2,1)} async-done(((bf16[288,256]{1,0:T(8,128)(2,1)}), bf16[2304,256]{1,0:T(8,128)(2,1)}) %all-gather.12.cloned.1.call-update) | async-done | bytes 1179664 | tf_op jit(solution)/shard_map/all_gather | solution.py:90
  202.2 3.6 gather_fusion.13
  207.3 3.5 gather_fusion.9
  212.9 3.5 gather_fusion.1
  218.6 3.6 gather_fusion.5
  224.3 3.5 gather_fusion.11
  229.9 3.5 gather_fusion.7
  246.0 3.6 copy.128
  249.6 3.7 copy.138
  265.3 8.0 %multiply_convert_fusion = (bf16[2,32,32,256]{3,2,1,0:T(8,128)(2,1)S(1)}, f32[2,32,32,256]{3,2,1,0:T(8,128)}) fusion(bf16[2,32,32,2304]{3,2,1,0:T(8,128)(2,1)} %slice_dynamic-update-slice_fusion, bf16[2304,256]{1,0:T(8,128)(2,1)} %all-gather.8.cloned.1.call-done), kind=kOutput, calls=%fused_computation.36 | convolution fusion | flops 2418540544 | bytes 13762560 | tf_op jit(solution)/shard_map/dot_general | solution.py:85
  273.5 9.9 %slice.204 = bf16[2,16,16,256]{3,2,1,0:T(8,128)(2,1)} slice(bf16[2,32,32,256]{3,2,1,0:T(8,128)(2,1)S(1)} %get-tuple-element.70), slice={[0:2:1], [0:32:2], [0:32:2], [0:256:1]} | slice | bytes 524288 | tf_op jit(solution)/shard_map/slice | solution.py:20
  283.4 9.8 %slice.205 = bf16[2,16,16,256]{3,2,1,0:T(8,128)(2,1)} slice(bf16[2,32,32,256]{3,2,1,0:T(8,128)(2,1)S(1)} %get-tuple-element.70), slice={[0:2:1], [0:32:2], [1:32:2], [0:256:1]} | slice | bytes 524288 | tf_op jit(solution)/shard_map/slice | solution.py:20
  293.2 9.8 %slice.207 = bf16[2,16,16,256]{3,2,1,0:T(8,128)(2,1)} slice(bf16[2,32,32,256]{3,2,1,0:T(8,128)(2,1)S(1)} %get-tuple-element.70), slice={[0:2:1], [1:32:2], [0:32:2], [0:256:1]} | slice | bytes 524288 | tf_op jit(solution)/shard_map/slice | solution.py:20
  303.0 9.8 %slice.208 = bf16[2,16,16,256]{3,2,1,0:T(8,128)(2,1)} slice(bf16[2,32,32,256]{3,2,1,0:T(8,128)(2,1)S(1)} %get-tuple-element.70), slice={[0:2:1], [1:32:2], [1:32:2], [0:256:1]} | slice | bytes 524288 | tf_op jit(solution)/shard_map/slice | solution.py:20
  320.9 7.9 %convolution_bitcast_fusion.1 = f32[2304,256]{1,0:T(8,128)} fusion(bf16[2,32,32,2304]{3,2,1,0:T(8,128)(2,1)} %slice_dynamic-update-slice_fusion, f32[2,32,32,256]{3,0,2,1:T(2,128)S(1)} %slice.308, f32[2,32,32,256]{3,2,1,0:T(8,128)S(1)} %copy-done.25), kind=kOutput, calls=%fused_computation.24 | convolution fusion | flops 2420637696 | bytes 15990784 | tf_op jit(solution)/shard_map/dot_general | solution.py:137
  328.8 64.2 %all-gather.10.cloned.1.call-done = bf16[64,2,32,256]{3,2,1,0:T(8,128)(2,1)} async-done(((bf16[2,2,32,256]{3,2,1,0:T(8,128)(2,1)}), bf16[64,2,32,256]{3,2,1,0:T(8,128)(2,1)}) %all-gather.10.cloned.1.call-update) | async-done | bytes 2097168 | tf_op jit(solution)/shard_map/all_gather | solution.py:94
  405.7 12.5 %slice.203 = bf16[2,16,16,256]{3,2,1,0:T(8,128)(2,1)S(1)} slice(bf16[2,32,33,256]{3,2,1,0:T(8,128)(2,1)} %pad_maximum_fusion.3), slice={[0:2:1], [0:32:2], [0:32:2], [0:256:1]} | slice | bytes 524288 | tf_op jit(solution)/shard_map/slice | solution.py:20
  418.3 12.5 %slice.206 = bf16[2,16,16,256]{3,2,1,0:T(8,128)(2,1)S(1)} slice(bf16[2,32,33,256]{3,2,1,0:T(8,128)(2,1)} %pad_maximum_fusion.3), slice={[0:2:1], [1:32:2], [0:32:2], [0:256:1]} | slice | bytes 524288 | tf_op jit(solution)/shard_map/slice | solution.py:20
  434.9 164.7 %all-reduce.6.cloned.1.call-done = (f32[2304,256]{1,0:T(8,128)}, f32[2304,256]{1,0:T(8,128)}) async-done(((f32[2304,256]{1,0:T(8,128)}, f32[2304,256]{1,0:T(8,128)}), (f32[2304,256]{1,0:T(8,128)}, f32[2304,256]{1,0:T(8,128)})) %all-reduce.6.cloned.1.call-update) | async-done | bytes 4718608 | tf_op jit(solution)/shard_map/psum | solution.py:144
  613.9 26.2 %reduce-scatter.9.cloned.1.call-done = f32[32,72]{1,0:T(8,128)} async-done(((f32[256,72]{1,0:T(8,128)}), f32[32,72]{1,0:T(8,128)}) %reduce-scatter.9.cloned.1.call-update) | async-done | bytes 9232
  640.2 34.8 %reduce-scatter.7.cloned.1.call-done = f32[32,72]{1,0:T(8,128)} async-done(((f32[256,72]{1,0:T(8,128)}), f32[32,72]{1,0:T(8,128)}) %reduce-scatter.7.cloned.1.call-update) | async-done | bytes 9232
  (193 shorter events, 105.9 us)
Async XLA Ops:
  7.2 81.6 %all-gather.14.cloned.1.call-start = ((), (), s32[]{:S(2)}) async-start(), calls=%async_computation.6 | async-start | bytes 1081344 | tf_op jit(solution)/shard_map/all_gather | solution.py:110
  8.9 188.7 %copy-start.3 = (bf16[2,16,16,256]{3,2,1,0:T(8,128)(2,1)}, bf16[2,16,16,256]{3,2,1,0:T(8,128)(2,1)S(1)}, u32[]{:S(2)}) copy-start(bf16[2,16,16,256]{3,2,1,0:T(8,128)(2,1)S(1)} %bitcast_multiply_fusion) | copy-start | bytes 786436
  9.7 161.4 %all-gather.6.cloned.1.call-start = ((), (), s32[]{:S(2)}) async-start(), calls=%async_computation.2 | async-start | bytes 4325376 | tf_op jit(solution)/shard_map/all_gather | solution.py:71
  12.4 185.3 %all-gather.12.cloned.1.call-start = ((), (), s32[]{:S(2)}) async-start(), calls=%async_computation.5 | async-start | bytes 1327104 | tf_op jit(solution)/shard_map/all_gather | solution.py:90
  13.1 252.2 %all-gather.8.cloned.1.call-start = ((), (), s32[]{:S(2)}) async-start(), calls=%async_computation.3 | async-start | bytes 1327104 | tf_op jit(solution)/shard_map/all_gather | solution.py:87
  13.7 379.4 %all-gather.10.cloned.1.call-start = ((), (), s32[]{:S(2)}) async-start(), calls=%async_computation.4 | async-start | bytes 2162688 | tf_op jit(solution)/shard_map/all_gather | solution.py:94
  41.7 52.8 %copy-start.20 = (pred[2]{0:T(512)(128)(4,1)}, pred[2]{0:T(512)(128)(4,1)S(1)}, u32[]{:S(2)}) copy-start(pred[2]{0:T(512)(128)(4,1)S(1)} %get-tuple-element.74) | copy-start | bytes 10
  42.9 51.4 %copy-start.21 = (bf16[2]{0:T(256)(128)(2,1)}, bf16[2]{0:T(256)(128)(2,1)S(1)}, u32[]{:S(2)}) copy-start(bf16[2]{0:T(256)(128)(2,1)S(1)} %get-tuple-element.78) | copy-start | bytes 16
  42.9 51.4 %copy-start.22 = (pred[2]{0:T(512)(128)(4,1)}, pred[2]{0:T(512)(128)(4,1)S(1)}, u32[]{:S(2)}) copy-start(pred[2]{0:T(512)(128)(4,1)S(1)} %get-tuple-element.41) | copy-start | bytes 10
  42.9 51.5 %copy-start.23 = (bf16[2]{0:T(256)(128)(2,1)}, bf16[2]{0:T(256)(128)(2,1)S(1)}, u32[]{:S(2)}) copy-start(bf16[2]{0:T(256)(128)(2,1)S(1)} %get-tuple-element.82) | copy-start | bytes 16
  43.0 51.4 %copy-start.14 = (s32[1024]{0:T(1024)}, s32[1024]{0:T(1024)S(1)}, u32[]{:S(2)}) copy-start(s32[1024]{0:T(1024)S(1)} %pad_clamp_fusion.2) | copy-start | bytes 12292
  43.0 49.4 %copy-start.13 = (s32[1024]{0:T(1024)}, s32[1024]{0:T(1024)S(1)}, u32[]{:S(2)}) copy-start(s32[1024]{0:T(1024)S(1)} %pad_clamp_fusion.6) | copy-start | bytes 12292
  202.2 39.3 %copy-start = (bf16[1,2,32,32,256]{4,3,2,1,0:T(8,128)(2,1)S(1)}, bf16[1,2,32,32,256]{4,3,2,1,0:T(8,128)(2,1)}, u32[]{:S(2)}) copy-start(bf16[1,2,32,32,256]{4,3,2,1,0:T(8,128)(2,1)} %param.14) | copy-start | bytes 3145732
  316.0 283.7 %all-reduce.6.cloned.1.call-start = ((), (), s32[]{:S(2)}) async-start(), calls=%async_computation.9 | async-start | bytes 9437184 | tf_op jit(solution)/shard_map/psum | solution.py:144
  320.9 74.4 %copy-start.19 = (pred[2]{0:T(512)(128)(4,1)S(1)}, pred[2]{0:T(512)(128)(4,1)}, u32[]{:S(2)}) copy-start(pred[2]{0:T(512)(128)(4,1)} %get-tuple-element.39) | copy-start | bytes 10
  320.9 74.5 %copy-start.17 = (bf16[2]{0:T(256)(128)(2,1)S(1)}, bf16[2]{0:T(256)(128)(2,1)}, u32[]{:S(2)}) copy-start(bf16[2]{0:T(256)(128)(2,1)} %get-tuple-element.81) | copy-start | bytes 16
  328.8 70.8 %copy-start.18 = (pred[2]{0:T(512)(128)(4,1)S(1)}, pred[2]{0:T(512)(128)(4,1)}, u32[]{:S(2)}) copy-start(pred[2]{0:T(512)(128)(4,1)} %get-tuple-element.33) | copy-start | bytes 10
  328.8 70.9 %copy-start.24 = (bf16[2]{0:T(256)(128)(2,1)S(1)}, bf16[2]{0:T(256)(128)(2,1)}, u32[]{:S(2)}) copy-start(bf16[2]{0:T(256)(128)(2,1)} %get-tuple-element.80) | copy-start | bytes 16
  328.8 73.2 %copy-start.15 = (pred[2]{0:T(512)(128)(4,1)S(1)}, pred[2]{0:T(512)(128)(4,1)}, u32[]{:S(2)}) copy-start(pred[2]{0:T(512)(128)(4,1)} %get-tuple-element.35) | copy-start | bytes 10
  328.8 73.3 %copy-start.16 = (bf16[2]{0:T(256)(128)(2,1)S(1)}, bf16[2]{0:T(256)(128)(2,1)}, u32[]{:S(2)}) copy-start(bf16[2]{0:T(256)(128)(2,1)} %get-tuple-element.76) | copy-start | bytes 16
  402.9 28.0 %copy-start.9 = (bf16[2,16,16,256]{3,2,1,0:T(8,128)(2,1)S(1)}, bf16[2,16,16,256]{3,2,1,0:T(8,128)(2,1)}, u32[]{:S(2)}) copy-start(bf16[2,16,16,256]{3,2,1,0:T(8,128)(2,1)} %slice.204) | copy-start | bytes 786436
  403.8 27.2 %copy-start.8 = (bf16[2,16,16,256]{3,2,1,0:T(8,128)(2,1)S(1)}, bf16[2,16,16,256]{3,2,1,0:T(8,128)(2,1)}, u32[]{:S(2)}) copy-start(bf16[2,16,16,256]{3,2,1,0:T(8,128)(2,1)} %slice.205) | copy-start | bytes 786436
  434.8 205.3 %reduce-scatter.9.cloned.1.call-start = ((), (), s32[]{:S(2)}) async-start(), calls=%async_computation.8 | async-start | bytes 147456
  608.4 66.6 %reduce-scatter.7.cloned.1.call-start = ((), (), s32[]{:S(2)}) async-start(), calls=%async_computation.7 | async-start | bytes 147456
  (10 other events, 67.1 us)
Sparse Core Ops, SparseCore 0:
  10.6 78.0 all-gather.13
  91.9 79.1 all-gather.5
  172.9 24.6 all-gather.11
  199.3 26.2 all-gather.7
  316.1 76.9 all-gather.9
  435.0 164.6 all-reduce.5
  608.5 31.5 reduce-scatter.8
  643.2 31.6 reduce-scatter.6
where the time goes:
time: 686 us; the launch traced here: 682 us
  waiting for transfers between devices  429 us (63%)
  local copies, waits for them, and re-layouts  143 us (21%)
  other arithmetic  46.8 us (7%)
  matrix products  23.9 us (3%)
  blocking collectives  22.6 us (3%)
  between operations  16.8 us (2%)
    psum x1, waiting for transfers between devices, local(): full_first, full_second = lax.psum((grad_first, grad_second), 'region')  165 us
    all_gather x1, waiting for transfers between devices, local(): all_edges = lax.all_gather(edge_rims, 'region', axis=0, tiled=True)  76.7 us
    slice x9, local copies, waits for them, and re-layouts, tap_patches(): padded[:, tap_row:tap_row + stride * out_side:stride, tap_col:tap_col + s...  67.2 us
    all_gather x1, waiting for transfers between devices, local(): all_hidden = lax.all_gather(hidden_rims, 'region', axis=0, tiled=True)  64.2 us
    unnamed x10, waiting for transfers between devices  62.3 us
    gather x22, local copies, waits for them, and re-layouts, fetch(): picked = jnp.take(all_rims, jnp.take(slot_of, position), axis=0)[:, which]  44.7 us
    all_gather x1, waiting for transfers between devices, local(): all_grads = lax.all_gather(grad_rims, 'region', axis=0, tiled=True)  37.8 us
    all_gather x1, waiting for transfers between devices, local(): second_full = lax.all_gather(w_second, 'scene', axis=0, tiled=True)  23.1 us
  transfers between devices with their start and end apart: 8, of which 7 were waited for; matrix products, arithmetic and copies ran while one was open for 16% of the time, Pallas kernels for 0%

commit v1 on v0

--- a/solution.py
+++ b/solution.py
@@ -87,7 +87,9 @@
         lax.all_gather(w_first, "scene", axis=0, tiled=True),
         preferred_element_type=jnp.float32,
     )
-    second_full = lax.all_gather(w_second, "scene", axis=0, tiled=True)
+    second_full = jnp.concatenate(
+        lax.all_to_all(jnp.stack([w_second] * lax.axis_size("scene")), "scene", 0, 0), axis=0
+    )
     pre_act = pre_flat.reshape(slot_count, tile_side, tile_side, channels)
     hidden = jax.nn.silu(pre_act).astype(jnp.bfloat16)
     hidden_rims = jnp.stack([hidden[:, tile_side - 1], hidden[:, :, tile_side - 1]], axis=1)

time: 686 us -> 661 us (0.964)
  waiting for transfers between devices: 429 us -> 400 us
    all_gather x1 -> x0, waiting for transfers between devices: 23.1 us -> none  [local(): second_full = lax.all_gather(w_second, 'scene', axis=0, tiled=True)]
    unnamed x10 -> x9, waiting for transfers between devices: 62.3 us -> 61.8 us
    unnamed x73 -> x79, local copies, waits for them, and re-layouts: 15.9 us -> 15.4 us
  transfers between devices with their start and end apart: 8 -> 8, of which waited for: 7 -> 6; matrix products, arithmetic and copies ran while one was open for 16% -> 17% of each run, Pallas kernels for 0% -> 0%
where the time goes in v1:
time: 661 us; the launch traced here: 657 us
  waiting for transfers between devices  400 us (61%)
  local copies, waits for them, and re-layouts  144 us (22%)
  other arithmetic  46.2 us (7%)
  blocking collectives  22.6 us (3%)
  matrix products  22.6 us (3%)
  between operations  16.8 us (3%)
    psum x1, waiting for transfers between devices, local(): full_first, full_second = lax.psum((grad_first, grad_second), 'region')  165 us
    all_gather x1, waiting for transfers between devices, local(): all_edges = lax.all_gather(edge_rims, 'region', axis=0, tiled=True)  76.6 us
    slice x9, local copies, waits for them, and re-layouts, tap_patches(): padded[:, tap_row:tap_row + stride * out_side:stride, tap_col:tap_col + s...  67.2 us
    all_gather x1, waiting for transfers between devices, local(): all_hidden = lax.all_gather(hidden_rims, 'region', axis=0, tiled=True)  62.7 us
    unnamed x9, waiting for transfers between devices  61.8 us
    gather x22, local copies, waits for them, and re-layouts, fetch(): picked = jnp.take(all_rims, jnp.take(slot_of, position), axis=0)[:, which]  44.7 us
    all_gather x1, waiting for transfers between devices, local(): all_grads = lax.all_gather(grad_rims, 'region', axis=0, tiled=True)  34 us
    unnamed x1, blocking collectives  22.6 us
  transfers between devices with their start and end apart: 8, of which 6 were waited for; matrix products, arithmetic and copies ran while one was open for 17% of the time, Pallas kernels for 0%

profile of v1, /device:TPU:8, one launch (start us, length us, event | category | flops | bytes accessed | tf_op | source)
XLA Modules:
  0.0 657.0 jit_solution(17143372769571012453)
XLA Ops:
  14.4 4.3 all-to-all-start
  21.5 22.6 %all-reduce.2 = s32[64]{0:T(128)S(1)} all-reduce(s32[64]{0:T(128)S(1)} %bitcast_dynamic-update-slice_fusion), channel_id=1, replica_groups=mesh['scene'=8,'region'=32] {'region'}, use_global_device_ids=true, to_apply=%add.2 | all-reduce | flops 64 | bytes 512
  54.7 34.0 %all-gather.11.cloned.1.call-done = bf16[64,2,16,256]{3,2,1,0:T(8,128)(2,1)} async-done(((bf16[2,2,16,256]{3,2,1,0:T(8,128)(2,1)}), bf16[64,2,16,256]{3,2,1,0:T(8,128)(2,1)}) %all-gather.11.cloned.1.call-update) | async-done | bytes 1048592 | tf_op jit(solution)/shard_map/all_gather | solution.py:112
  94.5 76.6 %all-gather.5.cloned.1.call-done = bf16[64,4,32,256]{3,2,1,0:T(8,128)(2,1)} async-done(((bf16[2,4,32,256]{3,2,1,0:T(8,128)(2,1)}), bf16[64,4,32,256]{3,2,1,0:T(8,128)(2,1)}) %all-gather.5.cloned.1.call-update) | async-done | bytes 4194320 | tf_op jit(solution)/shard_map/all_gather | solution.py:71
  179.0 3.6 gather_fusion.13
  184.0 3.5 gather_fusion.9
  189.7 3.5 gather_fusion.1
  195.3 3.6 gather_fusion.5
  201.0 3.5 gather_fusion.11
  206.6 3.5 gather_fusion.7
  222.7 3.6 copy.128
  226.2 3.7 copy.138
  242.1 8.0 %multiply_convert_fusion = (bf16[2,32,32,256]{3,2,1,0:T(8,128)(2,1)S(1)}, f32[2,32,32,256]{3,2,1,0:T(8,128)}) fusion(bf16[2,32,32,2304]{3,2,1,0:T(8,128)(2,1)} %slice_dynamic-update-slice_fusion, bf16[2304,256]{1,0:T(8,128)(2,1)} %all-gather.7.cloned.1.call-done), kind=kOutput, calls=%fused_computation.36 | convolution fusion | flops 2418540544 | bytes 13762560 | tf_op jit(solution)/shard_map/dot_general | solution.py:85
  250.2 9.9 %slice.204 = bf16[2,16,16,256]{3,2,1,0:T(8,128)(2,1)} slice(bf16[2,32,32,256]{3,2,1,0:T(8,128)(2,1)S(1)} %get-tuple-element.70), slice={[0:2:1], [0:32:2], [0:32:2], [0:256:1]} | slice | bytes 524288 | tf_op jit(solution)/shard_map/slice | solution.py:20
  260.1 9.8 %slice.205 = bf16[2,16,16,256]{3,2,1,0:T(8,128)(2,1)} slice(bf16[2,32,32,256]{3,2,1,0:T(8,128)(2,1)S(1)} %get-tuple-element.70), slice={[0:2:1], [0:32:2], [1:32:2], [0:256:1]} | slice | bytes 524288 | tf_op jit(solution)/shard_map/slice | solution.py:20
  269.9 9.8 %slice.207 = bf16[2,16,16,256]{3,2,1,0:T(8,128)(2,1)} slice(bf16[2,32,32,256]{3,2,1,0:T(8,128)(2,1)S(1)} %get-tuple-element.70), slice={[0:2:1], [1:32:2], [0:32:2], [0:256:1]} | slice | bytes 524288 | tf_op jit(solution)/shard_map/slice | solution.py:20
  279.7 9.8 %slice.208 = bf16[2,16,16,256]{3,2,1,0:T(8,128)(2,1)} slice(bf16[2,32,32,256]{3,2,1,0:T(8,128)(2,1)S(1)} %get-tuple-element.70), slice={[0:2:1], [1:32:2], [1:32:2], [0:256:1]} | slice | bytes 524288 | tf_op jit(solution)/shard_map/slice | solution.py:20
  297.6 7.9 %convolution_bitcast_fusion.1 = f32[2304,256]{1,0:T(8,128)} fusion(bf16[2,32,32,2304]{3,2,1,0:T(8,128)(2,1)} %slice_dynamic-update-slice_fusion, f32[2,32,32,256]{3,0,2,1:T(2,128)S(1)} %slice.308, f32[2,32,32,256]{3,2,1,0:T(8,128)S(1)} %copy-done.28), kind=kOutput, calls=%fused_computation.24 | convolution fusion | flops 2420637696 | bytes 15990784 | tf_op jit(solution)/shard_map/dot_general | solution.py:139
  305.6 62.7 %all-gather.9.cloned.1.call-done = bf16[64,2,32,256]{3,2,1,0:T(8,128)(2,1)} async-done(((bf16[2,2,32,256]{3,2,1,0:T(8,128)(2,1)}), bf16[64,2,32,256]{3,2,1,0:T(8,128)(2,1)}) %all-gather.9.cloned.1.call-update) | async-done | bytes 2097168 | tf_op jit(solution)/shard_map/all_gather | solution.py:96
  380.9 12.5 %slice.203 = bf16[2,16,16,256]{3,2,1,0:T(8,128)(2,1)S(1)} slice(bf16[2,32,33,256]{3,2,1,0:T(8,128)(2,1)} %pad_maximum_fusion.3), slice={[0:2:1], [0:32:2], [0:32:2], [0:256:1]} | slice | bytes 524288 | tf_op jit(solution)/shard_map/slice | solution.py:20
  393.5 12.5 %slice.206 = bf16[2,16,16,256]{3,2,1,0:T(8,128)(2,1)S(1)} slice(bf16[2,32,33,256]{3,2,1,0:T(8,128)(2,1)} %pad_maximum_fusion.3), slice={[0:2:1], [1:32:2], [0:32:2], [0:256:1]} | slice | bytes 524288 | tf_op jit(solution)/shard_map/slice | solution.py:20
  410.1 164.7 %all-reduce.6.cloned.1.call-done = (f32[2304,256]{1,0:T(8,128)}, f32[2304,256]{1,0:T(8,128)}) async-done(((f32[2304,256]{1,0:T(8,128)}, f32[2304,256]{1,0:T(8,128)}), (f32[2304,256]{1,0:T(8,128)}, f32[2304,256]{1,0:T(8,128)})) %all-reduce.6.cloned.1.call-update) | async-done | bytes 4718608 | tf_op jit(solution)/shard_map/psum | solution.py:146
  589.1 26.2 %reduce-scatter.9.cloned.1.call-done = f32[32,72]{1,0:T(8,128)} async-done(((f32[256,72]{1,0:T(8,128)}), f32[32,72]{1,0:T(8,128)}) %reduce-scatter.9.cloned.1.call-update) | async-done | bytes 9232
  615.3 34.8 %reduce-scatter.7.cloned.1.call-done = f32[32,72]{1,0:T(8,128)} async-done(((f32[256,72]{1,0:T(8,128)}), f32[32,72]{1,0:T(8,128)}) %reduce-scatter.7.cloned.1.call-update) | async-done | bytes 9232
  (199 shorter events, 105.3 us)
Async XLA Ops:
  7.2 81.6 %all-gather.11.cloned.1.call-start = ((), (), s32[]{:S(2)}) async-start(), calls=%async_computation.6 | async-start | bytes 1081344 | tf_op jit(solution)/shard_map/all_gather | solution.py:112
  8.9 165.7 %copy-start.5 = (bf16[2,16,16,256]{3,2,1,0:T(8,128)(2,1)}, bf16[2,16,16,256]{3,2,1,0:T(8,128)(2,1)S(1)}, u32[]{:S(2)}) copy-start(bf16[2,16,16,256]{3,2,1,0:T(8,128)(2,1)S(1)} %bitcast_multiply_fusion) | copy-start | bytes 786436
  9.6 161.5 %all-gather.5.cloned.1.call-start = ((), (), s32[]{:S(2)}) async-start(), calls=%async_computation.3 | async-start | bytes 4325376 | tf_op jit(solution)/shard_map/all_gather | solution.py:71
  14.4 160.2 %all-to-all-start = ((bf16[8,288,256]{2,1,0:T(8,128)(2,1)}), bf16[8,288,256]{2,1,0:T(8,128)(2,1)S(1)}, u32[]{:S(2)}, u32[]{:S(2)}) async-start(bf16[8,288,256]{2,1,0:T(8,128)(2,1)} %stack.34), calls=%async_computation | async-start | bytes 2359296 | tf_op jit(solution)/shard_map/all_to_all | solution.py:91
  18.7 223.4 %all-gather.7.cloned.1.call-start = ((), (), s32[]{:S(2)}) async-start(), calls=%async_computation.4 | async-start | bytes 1327104 | tf_op jit(solution)/shard_map/all_gather | solution.py:87
  19.4 348.8 %all-gather.9.cloned.1.call-start = ((), (), s32[]{:S(2)}) async-start(), calls=%async_computation.5 | async-start | bytes 2162688 | tf_op jit(solution)/shard_map/all_gather | solution.py:96
  45.5 48.9 %copy-start.21 = (pred[2]{0:T(512)(128)(4,1)}, pred[2]{0:T(512)(128)(4,1)S(1)}, u32[]{:S(2)}) copy-start(pred[2]{0:T(512)(128)(4,1)S(1)} %get-tuple-element.74) | copy-start | bytes 10
  46.8 47.6 %copy-start.22 = (bf16[2]{0:T(256)(128)(2,1)}, bf16[2]{0:T(256)(128)(2,1)S(1)}, u32[]{:S(2)}) copy-start(bf16[2]{0:T(256)(128)(2,1)S(1)} %get-tuple-element.78) | copy-start | bytes 16
  46.8 47.6 %copy-start.23 = (pred[2]{0:T(512)(128)(4,1)}, pred[2]{0:T(512)(128)(4,1)S(1)}, u32[]{:S(2)}) copy-start(pred[2]{0:T(512)(128)(4,1)S(1)} %get-tuple-element.41) | copy-start | bytes 10
  46.8 47.6 %copy-start.24 = (bf16[2]{0:T(256)(128)(2,1)}, bf16[2]{0:T(256)(128)(2,1)S(1)}, u32[]{:S(2)}) copy-start(bf16[2]{0:T(256)(128)(2,1)S(1)} %get-tuple-element.82) | copy-start | bytes 16
  46.8 47.6 %copy-start.15 = (s32[1024]{0:T(1024)}, s32[1024]{0:T(1024)S(1)}, u32[]{:S(2)}) copy-start(s32[1024]{0:T(1024)S(1)} %pad_clamp_fusion.2) | copy-start | bytes 12292
  46.8 45.5 %copy-start.14 = (s32[1024]{0:T(1024)}, s32[1024]{0:T(1024)S(1)}, u32[]{:S(2)}) copy-start(s32[1024]{0:T(1024)S(1)} %pad_clamp_fusion.6) | copy-start | bytes 12292
  179.0 39.3 %copy-start = (bf16[1,2,32,32,256]{4,3,2,1,0:T(8,128)(2,1)S(1)}, bf16[1,2,32,32,256]{4,3,2,1,0:T(8,128)(2,1)}, u32[]{:S(2)}) copy-start(bf16[1,2,32,32,256]{4,3,2,1,0:T(8,128)(2,1)} %param.14) | copy-start | bytes 3145732
  292.7 282.1 %all-reduce.6.cloned.1.call-start = ((), (), s32[]{:S(2)}) async-start(), calls=%async_computation.9 | async-start | bytes 9437184 | tf_op jit(solution)/shard_map/psum | solution.py:146
  297.6 72.9 %copy-start.20 = (pred[2]{0:T(512)(128)(4,1)S(1)}, pred[2]{0:T(512)(128)(4,1)}, u32[]{:S(2)}) copy-start(pred[2]{0:T(512)(128)(4,1)} %get-tuple-element.39) | copy-start | bytes 10
  297.6 73.0 %copy-start.18 = (bf16[2]{0:T(256)(128)(2,1)S(1)}, bf16[2]{0:T(256)(128)(2,1)}, u32[]{:S(2)}) copy-start(bf16[2]{0:T(256)(128)(2,1)} %get-tuple-element.81) | copy-start | bytes 16
  305.6 69.3 %copy-start.19 = (pred[2]{0:T(512)(128)(4,1)S(1)}, pred[2]{0:T(512)(128)(4,1)}, u32[]{:S(2)}) copy-start(pred[2]{0:T(512)(128)(4,1)} %get-tuple-element.33) | copy-start | bytes 10
  305.6 69.4 %copy-start.25 = (bf16[2]{0:T(256)(128)(2,1)S(1)}, bf16[2]{0:T(256)(128)(2,1)}, u32[]{:S(2)}) copy-start(bf16[2]{0:T(256)(128)(2,1)} %get-tuple-element.80) | copy-start | bytes 16
  305.6 71.7 %copy-start.16 = (pred[2]{0:T(512)(128)(4,1)S(1)}, pred[2]{0:T(512)(128)(4,1)}, u32[]{:S(2)}) copy-start(pred[2]{0:T(512)(128)(4,1)} %get-tuple-element.35) | copy-start | bytes 10
  305.6 71.7 %copy-start.17 = (bf16[2]{0:T(256)(128)(2,1)S(1)}, bf16[2]{0:T(256)(128)(2,1)}, u32[]{:S(2)}) copy-start(bf16[2]{0:T(256)(128)(2,1)} %get-tuple-element.76) | copy-start | bytes 16
  378.1 28.0 %copy-start.10 = (bf16[2,16,16,256]{3,2,1,0:T(8,128)(2,1)S(1)}, bf16[2,16,16,256]{3,2,1,0:T(8,128)(2,1)}, u32[]{:S(2)}) copy-start(bf16[2,16,16,256]{3,2,1,0:T(8,128)(2,1)} %slice.204) | copy-start | bytes 786436
  379.0 27.2 %copy-start.9 = (bf16[2,16,16,256]{3,2,1,0:T(8,128)(2,1)S(1)}, bf16[2,16,16,256]{3,2,1,0:T(8,128)(2,1)}, u32[]{:S(2)}) copy-start(bf16[2,16,16,256]{3,2,1,0:T(8,128)(2,1)} %slice.205) | copy-start | bytes 786436
  410.0 205.3 %reduce-scatter.9.cloned.1.call-start = ((), (), s32[]{:S(2)}) async-start(), calls=%async_computation.8 | async-start | bytes 147456
  583.5 66.6 %reduce-scatter.7.cloned.1.call-start = ((), (), s32[]{:S(2)}) async-start(), calls=%async_computation.7 | async-start | bytes 147456
  (13 other events, 86.7 us)
Sparse Core Ops, SparseCore 0:
  10.6 78.0 all-gather.10
  91.9 79.1 all-gather.4
  172.9 24.6 all-gather.6
  292.8 75.4 all-gather.8
  410.1 164.5 all-reduce.5
  583.7 31.5 reduce-scatter.8
  618.4 31.6 reduce-scatter.6
